TPU v7x, 32 devices: a whole 2x2x4 slice. The times are simulated.
32 devices in a mesh: dom: 32 (over z, y, x, core).
Axes of the slice: x: 2, y: 2, z: 4, core: 2. Of those that a mesh axis runs over, the one named last changes fastest.
Arguments:
- coef_init: float32 [1024, 128], P('dom'), may hold values from -6 to 6
- basis: bfloat16 [49152, 1024], P('dom'), may hold values from -0.375 to 0.375
- basis_scale: float32 [384], P('dom'), may hold values from 0.5 to 2
- ext_force: float32 [49152, 128], P('dom'), may hold values from -6 to 6
- precond: float32 [1024], P('dom'), may hold values from 0.5 to 6, as said below
- connectivity: int32 [14400, 8], P('dom'), may hold values from 0 to 767, as said below
- halo_nodes: int32 [8192], P('dom'), may hold values from 0 to 511, as said below
- plastic: int32 [14400], P('dom'), may hold values 0 or 1
Outputs:
- coef_final: float32 [1024, 128], P('dom')
- nodal_residual: float32 [49152, 128], P('dom')
Inputs may be any that keep to these rules, and one draw needn't show every extreme that they name: `connectivity`: each part is a structured block of 16 x 16 x 2 nodes, numbered in a part-specific order; each row lists an element's 8 corners in corner-bit order (bit 0 along x, bit 1 along y, bit 2 along z). Entries below 512 are the part's own nodes; an entry 512 + h names the node listed h-th in the next part's halo_nodes (the next part's first z layer). `halo_nodes`: the entries of one part are its own local node numbers of its first z layer, in grid order with x fastest, all distinct. `precond`: Positive.
All inputs are finite; a program needn't handle non-finite values. No bound on the sum of `plastic` on one device may be relied on, other than what follows from the above.
Results may differ from a plain program's by a relative error of at most 0.0087.
Values may be sent and summed in bfloat16 or wider, within the bound.
No kernel may reach another device: no remote copies, remote signals or barrier semaphores. Data moves between devices by JAX's collectives and lax.ppermute only.
A program may use at most 64 MiB of HBM per device.

v0:
```python
import jax
import jax.numpy as jnp
from jax import lax
from jax.sharding import PartitionSpec as P

R = 1024
ITERS = 2
STEP_SIZE = 0.5
SHEAR_MODULUS = 1.0
LAME_FIRST = 1.5
HARDENING = 0.5
YIELD_STRESS = 3.0
EPSILON = 1e-05


def from_behind(value, axis, steps):
    count = lax.axis_size(axis)
    leading, last = (max(0, -steps), min(count, count - steps))
    return lax.ppermute(value, axis, [(source, source + steps) for source in range(leading, last)])


def corner_table():
    corner_bits = jnp.arange(8)[:, None] >> jnp.arange(3)[None, :] & 1
    return (2.0 * corner_bits.astype(jnp.float32) - 1.0) / 4.0


def element_forces(corner_disp, flags, corners):
    gradient = jnp.einsum("eaic,aj->eijc", corner_disp, corners, precision=lax.Precision.HIGHEST)
    strain = 0.5 * (gradient + jnp.swapaxes(gradient, 1, 2))
    volumetric = strain[:, 0, 0] + strain[:, 1, 1] + strain[:, 2, 2]
    identity = jnp.eye(3, dtype=jnp.float32)[None, :, :, None]
    shear_part = 2.0 * SHEAR_MODULUS * (strain - volumetric[:, None, None] / 3.0 * identity)
    magnitude = jnp.sqrt(jnp.sum(shear_part * shear_part, axis=(1, 2)))
    total_modulus = 2.0 * SHEAR_MODULUS + HARDENING
    plastic_factor = HARDENING / total_modulus + 2.0 * SHEAR_MODULUS * YIELD_STRESS / (
        total_modulus * jnp.maximum(magnitude, YIELD_STRESS)
    )
    factor = jnp.where(flags[:, None] == 1, plastic_factor, jnp.ones_like(plastic_factor))
    stress = LAME_FIRST * volumetric[:, None, None] * identity + factor[:, None, None] * shear_part
    return jnp.einsum("eijc,aj->eaic", stress, corners, precision=lax.Precision.HIGHEST)


def apply_scale(values, scales):
    return (values.reshape(scales.shape[0], -1, values.shape[-1]) * scales[:, None, None]).reshape(
        values.shape
    )


def on_device(coef_init, basis, basis_scale, ext_force, precond, connectivity, halo_nodes, plastic):
    rows_dev, cases = ext_force.shape
    node_count = rows_dev // 3
    halo_count = halo_nodes.shape[0]
    owned_rows = coef_init.shape[0]
    corners = corner_table()
    node_ids = jnp.arange(node_count + halo_count, dtype=jnp.int32)
    incidence = (node_ids[:, None] == connectivity.reshape(-1)[None, :]).astype(jnp.float32)
    nodal_residual = ext_force
    coef_full, precond_full = (
        lax.all_gather(coef_init, "dom", axis=0, tiled=True),
        lax.all_gather(precond, "dom", axis=0, tiled=True),
    )
    for sweep in range(ITERS):
        lifted = jnp.dot(basis, coef_full.astype(jnp.bfloat16), preferred_element_type=jnp.float32)
        nodes = apply_scale(lifted, basis_scale).reshape(node_count, 3, cases)
        outgoing = nodes[halo_nodes]
        incoming = from_behind(outgoing, "dom", -1)
        extended = jnp.concatenate([nodes, incoming], axis=0)
        corner_force = element_forces(extended[connectivity], plastic, corners)
        internal = jnp.dot(
            incidence,
            corner_force.reshape(-1, 3 * cases),
            precision=lax.Precision.HIGHEST,
            preferred_element_type=jnp.float32,
        ).reshape(node_count + halo_count, 3, cases)
        returned = from_behind(internal[node_count:], "dom", 1)
        own_force = internal[:node_count].at[halo_nodes].add(returned)
        nodal_residual = ext_force - own_force.reshape(rows_dev, cases)
        scaled = apply_scale(nodal_residual, basis_scale).astype(jnp.bfloat16)
        partial_sum = lax.dot_general(
            basis, scaled, (((0,), (0,)), ((), ())), preferred_element_type=jnp.float32
        )
        reduced = lax.psum(partial_sum, "dom")
        update = precond_full[:, None] * reduced
        root_mean = jnp.sqrt(jnp.sum(update * update, axis=0) / R + EPSILON)
        coef_full = coef_full + STEP_SIZE * update / root_mean
    coef_out = lax.dynamic_slice_in_dim(
        coef_full, lax.axis_index("dom") * owned_rows, owned_rows, 0
    )
    return (coef_out, nodal_residual)


def solution(mesh):
    return jax.shard_map(
        on_device,
        mesh=mesh,
        in_specs=(
            P("dom", None),
            P("dom", None),
            P("dom"),
            P("dom", None),
            P("dom"),
            P("dom", None),
            P("dom"),
            P("dom"),
        ),
        out_specs=(P("dom", None), P("dom", None)),
        check_vma=False,
    )
```

profile of v0, /device:TPU:0, one launch (start us, length us, event | category | flops | bytes accessed | tf_op | source)
XLA Modules:
  0.0 553.9 jit_solution(8672493367761439965)
XLA Ops:
  7.2 45.1 %all_gather.6 = f32[1024,128]{1,0:T(8,128)S(1)} all-gather(f32[32,128]{1,0:T(8,128)} %param.8), channel_id=1, replica_groups=mesh['dom'=32] {'dom'}, dimensions={0}, use_global_device_ids=true | all-gather | bytes 540672 | tf_op jit(solution)/shard_map/all_gather | solution.py:59
  52.3 0.8 copy-done.1
  53.1 1.9 fusion.15
  55.0 2.3 reshape.100
  57.7 2.8 broadcast_multiply_fusion.1
  60.5 3.0 gather_fusion
  63.5 1.3 collective-permute-start
  64.8 0.8 copy.36
  65.6 0.8 copy.37
  66.4 1.1 reshape.116
  67.5 1.1 eq.35
  68.7 3.0 pad_maximum_fusion
  71.6 14.1 %gather_fusion.1 = f32[3600,3,128]{2,1,0:T(4,128)} fusion(f32[768,3,128]{2,1,0:T(4,128)} %pad_maximum_fusion, s32[4096]{0:T(1024)S(1)} %pad_clamp_fusion), kind=kCustom, calls=%fused_computation.1 | custom fusion | bytes 11073600 | tf_op jit(solution)/shard_map/gather | solution.py:68
  85.8 8.2 %fusion.6 = f32[3,450,3,128]{3,0,2,1:T(4,128)S(1)} fusion(f32[450,8,3,128]{3,2,1,0:T(4,128)} %bitcast.78), kind=kOutput, calls=%fused_computation.15 | convolution fusion | flops 49766544 | bytes 7603200 | tf_op jit(solution)/shard_map/eaic,aj->eijc/dot_general | solution.py:28
  94.0 1.1 fusion.9
  95.9 2.2 multiply_reduce_fusion.1
  98.3 4.6 multiply_add_fusion.1
  102.9 6.6 %convolution_bitcast_fusion.1 = f32[3600,384]{1,0:T(8,128)S(1)} fusion(f32[450,3,3,128]{3,1,2,0:T(4,128)S(1)} %multiply_add_fusion.1), kind=kOutput, calls=%fused_computation.10 | convolution fusion | flops 49766544 | bytes 7603200 | tf_op jit(solution)/shard_map/eijc,aj->eaic/dot_general | solution.py:40
  109.5 8.3 %fusion.1 = f32[768,384]{0,1:T(8,128)S(1)} fusion(f32[3600,384]{1,0:T(8,128)S(1)} %convolution_bitcast_fusion.1, s32[3600]{0:T(1024)S(1)} %eq.35), kind=kOutput, calls=%fused_computation.8 | convolution fusion | flops 12742963200 | bytes 6723648 | tf_op jit(solution)/shard_map/dot_general | solution.py:69
  117.8 1.0 copy-done.4
  118.8 0.8 slice.68
  119.6 2.0 copy.42
  121.6 8.7 %collective-permute-start.1 = (f32[256,3,128]{2,1,0:T(4,128)}, f32[256,3,128]{2,1,0:T(4,128)}, u32[]{:S(2)}, u32[]{:S(2)}) collective-permute-start(f32[256,3,128]{2,1,0:T(4,128)} %copy.42), channel_id=1, source_target_pairs={{0,1},{1,2},{2,3},{3,4},{4,5},{5,6},{6,7},{7,8},{8,9},{9,10},{10,1... | collective-permute-start | bytes 1179656 | tf_op jit(solution)/shard_map/ppermute | solution.py:19
  130.3 2.1 slice.67
  132.4 2.5 copy.43
  134.8 26.6 %scatter_fusion = f32[512,3,128]{2,1,0:T(4,128)} fusion(f32[512,3,128]{2,1,0:T(4,128)} %copy.43, s32[256]{0:T(256)S(1)} %compare_select_fusion.1, f32[256,3,128]{2,1,0:T(4,128)} %collective-permute-done.1), kind=kCustom, calls=%fused_computation.4 | custom fusion | flops 98304 | bytes 1180672 | tf_op jit(solution)/shard_map/scatter-add | solution.py:76
  161.4 2.3 reshape.102
  163.7 3.2 convolution_bitcast_fusion.4
  166.9 2.0 copy.44
  169.2 38.4 %all-reduce = f32[1024]{0:T(1024)S(1)} all-reduce(f32[1024]{0:T(1024)S(1)} %dynamic-update-slice), channel_id=1, replica_groups=mesh['dom'=32] {'dom'}, use_global_device_ids=true, to_apply=%add | all-reduce | flops 1024 | bytes 8192
  207.6 87.8 %all-reduce.4.cloned.1.call-done = f32[1024,128]{0,1:T(8,128)} async-done(((f32[1024,128]{0,1:T(8,128)}), f32[1024,128]{0,1:T(8,128)}) %all-reduce.4.cloned.1.call-update) | async-done | bytes 524304 | tf_op jit(solution)/shard_map/psum | solution.py:82
  295.3 1.2 multiply_reduce_fusion.3
  296.5 1.3 divide_add_fusion
  297.9 0.8 copy-done.3
  298.7 2.1 convolution_bitcast_fusion.2
  300.7 2.3 copy.45
  303.1 2.3 reshape.103
  305.4 2.8 broadcast_multiply_fusion
  308.2 3.0 gather_fusion.2
  311.2 1.3 collective-permute-start.2
  312.5 2.7 collective-permute-done.2
  315.2 2.8 pad_maximum_fusion.1
  318.0 14.1 %gather_fusion.3 = f32[3600,3,128]{2,1,0:T(4,128)} fusion(f32[768,3,128]{2,1,0:T(4,128)} %pad_maximum_fusion.1, s32[4096]{0:T(1024)S(1)} %pad_clamp_fusion), kind=kCustom, calls=%fused_computation.3 | custom fusion | bytes 11073600 | tf_op jit(solution)/shard_map/gather | solution.py:68
  332.2 8.2 %fusion.4 = f32[3,450,3,128]{3,0,2,1:T(4,128)S(1)} fusion(f32[450,8,3,128]{3,2,1,0:T(4,128)} %bitcast.77), kind=kOutput, calls=%fused_computation.13 | convolution fusion | flops 49766544 | bytes 7603200 | tf_op jit(solution)/shard_map/eaic,aj->eijc/dot_general | solution.py:28
  340.4 1.1 fusion.8
  341.4 0.6 broadcast_multiply_fusion.5
  342.3 2.3 multiply_reduce_fusion
  344.7 4.6 multiply_add_fusion
  349.3 6.6 %convolution_bitcast_fusion = f32[3600,384]{1,0:T(8,128)S(1)} fusion(f32[450,3,3,128]{3,1,2,0:T(4,128)S(1)} %multiply_add_fusion), kind=kOutput, calls=%fused_computation.9 | convolution fusion | flops 49766544 | bytes 7603200 | tf_op jit(solution)/shard_map/eijc,aj->eaic/dot_general | solution.py:40
  355.9 8.3 %fusion = f32[768,384]{0,1:T(8,128)S(1)} fusion(f32[3600,384]{1,0:T(8,128)S(1)} %convolution_bitcast_fusion, s32[3600]{0:T(1024)S(1)} %eq.35), kind=kOutput, calls=%fused_computation.7 | convolution fusion | flops 12742963200 | bytes 6723648 | tf_op jit(solution)/shard_map/dot_general | solution.py:69
  364.2 1.0 copy-done.5
  365.3 1.0 copy.50
  366.3 9.3 %collective-permute-start.3 = (f32[256,3,128]{2,1,0:T(4,128)}, f32[256,3,128]{2,1,0:T(4,128)}, u32[]{:S(2)}, u32[]{:S(2)}) collective-permute-start(f32[256,3,128]{2,1,0:T(4,128)} %copy.50), channel_id=1, source_target_pairs={{0,1},{1,2},{2,3},{3,4},{4,5},{5,6},{6,7},{7,8},{8,9},{9,10},{10,1... | collective-permute-start | bytes 1179656 | tf_op jit(solution)/shard_map/ppermute | solution.py:19
  375.5 2.1 slice.72
  377.6 2.5 copy.51
  380.0 26.4 %scatter_fusion.1 = f32[512,3,128]{2,1,0:T(4,128)} fusion(f32[512,3,128]{2,1,0:T(4,128)} %copy.51, s32[256]{0:T(256)S(1)} %compare_select_fusion.1, f32[256,3,128]{2,1,0:T(4,128)} %collective-permute-done.3), kind=kCustom, calls=%fused_computation.5 | custom fusion | flops 98304 | bytes 1180672 | tf_op jit(solution)/shard_map/scatter-add | solution.py:76
  406.4 2.3 reshape.105
  408.7 1.5 sub.25
  410.1 0.9 copy-done.2
  411.0 1.8 convolution_bitcast_fusion.3
  412.8 131.2 %all-reduce.6.cloned.1.call-done = f32[1024,128]{0,1:T(8,128)} async-done(((f32[1024,128]{0,1:T(8,128)}), f32[1024,128]{0,1:T(8,128)}) %all-reduce.6.cloned.1.call-update) | async-done | bytes 524304 | tf_op jit(solution)/shard_map/psum | solution.py:82
  544.0 1.2 multiply_reduce_fusion.2
  545.2 1.0 dynamic-slice_add_fusion
  546.2 0.7 copy.52
  (46 shorter events, 2.2 us)
Async XLA Ops:
  7.2 46.0 %copy-start = (bf16[1536,1024]{1,0:T(8,128)(2,1)S(1)}, bf16[1536,1024]{1,0:T(8,128)(2,1)}, u32[]{:S(2)}) copy-start(bf16[1536,1024]{1,0:T(8,128)(2,1)} %param.9) | copy-start | bytes 9437188
  7.2 288.1 %all-reduce.4.cloned.1.call-start = ((), (), s32[]{:S(2)}) async-start(), calls=%async_computation | async-start | bytes 1048576 | tf_op jit(solution)/shard_map/psum | solution.py:82
  52.3 0.8 copy-start.1
  53.1 4.2 copy-start.7
  53.1 4.5 copy-start.9
  55.0 9.8 %copy-start.6 = (s32[450,8]{0,1:T(8,128)S(1)}, s32[450,8]{0,1:T(8,128)}, u32[]{:S(2)}) copy-start(s32[450,8]{0,1:T(8,128)} %param.13) | copy-start | bytes 43204
  57.3 11.3 %copy-start.8 = (s32[450]{0:T(512)S(1)}, s32[450]{0:T(512)}, u32[]{:S(2)}) copy-start(s32[450]{0:T(512)} %param.15) | copy-start | bytes 5404
  63.5 5.2 collective-permute-start
  117.8 1.0 copy-start.4
  121.6 13.3 %collective-permute-start.1 = (f32[256,3,128]{2,1,0:T(4,128)}, f32[256,3,128]{2,1,0:T(4,128)}, u32[]{:S(2)}, u32[]{:S(2)}) collective-permute-start(f32[256,3,128]{2,1,0:T(4,128)} %copy.42), channel_id=1, source_target_pairs={{0,1},{1,2},{2,3},{3,4},{4,5},{5,6},{6,7},{7,8},{8,9},{9,10},{10,1... | collective-permute-start | bytes 1179656 | tf_op jit(solution)/shard_map/ppermute | solution.py:19
  163.7 5.3 copy-start.10
  166.9 377.2 %all-reduce.6.cloned.1.call-start = ((), (), s32[]{:S(2)}) async-start(), calls=%async_computation.1 | async-start | bytes 1048576 | tf_op jit(solution)/shard_map/psum | solution.py:82
  297.8 0.8 copy-start.3
  311.2 4.0 collective-permute-start.2
  364.2 1.0 copy-start.5
  366.3 13.8 %collective-permute-start.3 = (f32[256,3,128]{2,1,0:T(4,128)}, f32[256,3,128]{2,1,0:T(4,128)}, u32[]{:S(2)}, u32[]{:S(2)}) collective-permute-start(f32[256,3,128]{2,1,0:T(4,128)} %copy.50), channel_id=1, source_target_pairs={{0,1},{1,2},{2,3},{3,4},{4,5},{5,6},{6,7},{7,8},{8,9},{9,10},{10,1... | collective-permute-start | bytes 1179656 | tf_op jit(solution)/shard_map/ppermute | solution.py:19
  410.1 0.9 copy-start.2
Sparse Core Ops, SparseCore 0:
  167.0 128.2 all-reduce.3
  413.0 131.0 all-reduce.5
where the time goes:
time: 564 us; the launch traced here: 554 us
  waiting for transfers between devices  222 us (39%)
  other arithmetic  88.2 us (16%)
  blocking collectives  83.5 us (15%)
  local copies, waits for them, and re-layouts  70.3 us (12%)
  matrix products  55.1 us (10%)
  starting transfers between devices  20.6 us (4%)
  between operations  14.6 us (3%)
    psum x2, waiting for transfers between devices, on_device(): reduced = lax.psum(partial_sum, 'dom')  219 us
    scatter-add x2, other arithmetic, on_device(): own_force = internal[:node_count].at[halo_nodes].add(returned)  52.9 us
    all_gather x1, blocking collectives, on_device(): lax.all_gather(coef_init, 'dom', axis=0, tiled=True)  45.1 us
    unnamed x1, blocking collectives  38.4 us
    gather x2, local copies, waits for them, and re-layouts, on_device(): corner_force = element_forces(extended[connectivity], plastic, corners)  28.3 us
    ppermute x4, starting transfers between devices, from_behind(): lax.ppermute(value, axis, [(source, source + steps) for source in range(l...  20.5 us
    dot_general x2, matrix products, on_device(): jnp.dot(incidence, corner_force.reshape(-1, 3 * cases), precision=lax.Pre...  16.7 us
    dot_general x2, matrix products, element_forces(): jnp.einsum('eaic,aj->eijc', corner_disp, corners, precision=lax.Precision...  16.4 us
  transfers between devices with their start and end apart: 6, of which 3 were waited for; matrix products, arithmetic and copies ran while one was open for 3% of the time, Pallas kernels for 0%

commit v1 on v0

--- a/solution.py
+++ b/solution.py
@@ -79,7 +79,7 @@
         partial_sum = lax.dot_general(
             basis, scaled, (((0,), (0,)), ((), ())), preferred_element_type=jnp.float32
         )
-        reduced = lax.psum(partial_sum, "dom")
+        reduced = jnp.sum(lax.all_gather(partial_sum, "dom"), axis=0)
         update = precond_full[:, None] * reduced
         root_mean = jnp.sqrt(jnp.sum(update * update, axis=0) / R + EPSILON)
         coef_full = coef_full + STEP_SIZE * update / root_mean

time: 564 us -> 593 us (1.051)
  local copies, waits for them, and re-layouts: 70.3 us -> 106 us
  waiting for transfers between devices: 222 us -> 191 us
  other arithmetic: 88.2 us -> 109 us
    psum x2 -> x0, waiting for transfers between devices: 219 us -> none  [on_device(): reduced = lax.psum(partial_sum, 'dom')]
    all_gather x0 -> x2, waiting for transfers between devices: none -> 189 us  [on_device(): reduced = jnp.sum(lax.all_gather(partial_sum, 'dom'), axis=0)]
    unnamed x29, local copies, waits for them, and re-layouts: 6.35 us -> 41.6 us
    reduce_sum x0 -> x2, other arithmetic: none -> 19.6 us  [on_device(): reduced = jnp.sum(lax.all_gather(partial_sum, 'dom'), axis=0)]
where the time goes in v1:
time: 593 us; the launch traced here: 582 us
  waiting for transfers between devices  191 us (32%)
  other arithmetic  109 us (18%)
  local copies, waits for them, and re-layouts  106 us (18%)
  blocking collectives  85.4 us (14%)
  matrix products  55.3 us (9%)
  starting transfers between devices  21 us (4%)
  between operations  14.6 us (2%)
    all_gather x2, waiting for transfers between devices, on_device(): reduced = jnp.sum(lax.all_gather(partial_sum, 'dom'), axis=0)  189 us
    scatter-add x2, other arithmetic, on_device(): own_force = internal[:node_count].at[halo_nodes].add(returned)  53.1 us
    all_gather x1, blocking collectives, on_device(): lax.all_gather(coef_init, 'dom', axis=0, tiled=True)  44.9 us
    unnamed x29, local copies, waits for them, and re-layouts  41.6 us
    unnamed x1, blocking collectives  40.5 us
    gather x2, local copies, waits for them, and re-layouts, on_device(): corner_force = element_forces(extended[connectivity], plastic, corners)  28 us
    ppermute x4, starting transfers between devices, from_behind(): lax.ppermute(value, axis, [(source, source + steps) for source in range(l...  20.9 us
    reduce_sum x2, other arithmetic, on_device(): reduced = jnp.sum(lax.all_gather(partial_sum, 'dom'), axis=0)  19.6 us
  transfers between devices with their start and end apart: 6, of which 3 were waited for; matrix products, arithmetic and copies ran while one was open for 3% of the time, Pallas kernels for 0%

profile of v1, /device:TPU:0, one launch (start us, length us, event | category | flops | bytes accessed | tf_op | source)
XLA Modules:
  0.0 582.5 jit_solution(891808664279036132)
XLA Ops:
  7.2 0.8 compare_select_fusion.1
  9.1 44.9 %all_gather.18 = f32[1024,128]{1,0:T(8,128)S(1)} all-gather(f32[32,128]{1,0:T(8,128)} %param.8), channel_id=1, replica_groups=mesh['dom'=32] {'dom'}, dimensions={0}, use_global_device_ids=true | all-gather | bytes 540672 | tf_op jit(solution)/shard_map/all_gather | solution.py:59
  54.8 1.9 fusion.15
  56.7 2.3 reshape.100
  59.0 2.8 broadcast_multiply_fusion.1
  61.8 3.0 gather_fusion
  64.8 1.3 collective-permute-start
  66.1 0.8 copy.49
  67.0 0.8 copy.50
  67.8 1.1 reshape.116
  68.9 1.1 eq.35
  70.0 3.0 pad_maximum_fusion
  73.0 13.9 %gather_fusion.1 = f32[3600,3,128]{2,1,0:T(4,128)} fusion(f32[768,3,128]{2,1,0:T(4,128)} %pad_maximum_fusion, s32[4096]{0:T(1024)S(1)} %pad_clamp_fusion), kind=kCustom, calls=%fused_computation.1 | custom fusion | bytes 11073600 | tf_op jit(solution)/shard_map/gather | solution.py:68
  86.8 8.2 %fusion.6 = f32[3,450,3,128]{3,0,2,1:T(4,128)S(1)} fusion(f32[450,8,3,128]{3,2,1,0:T(4,128)} %bitcast.88), kind=kOutput, calls=%fused_computation.17 | convolution fusion | flops 49766544 | bytes 7603200 | tf_op jit(solution)/shard_map/eaic,aj->eijc/dot_general | solution.py:28
  95.0 1.1 fusion.9
  97.0 2.2 multiply_reduce_fusion.1
  99.4 4.6 multiply_add_fusion.1
  103.9 6.8 %convolution_bitcast_fusion.1 = f32[3600,384]{1,0:T(8,128)S(1)} fusion(f32[450,3,3,128]{3,1,2,0:T(4,128)S(1)} %multiply_add_fusion.1), kind=kOutput, calls=%fused_computation.12 | convolution fusion | flops 49766544 | bytes 7603200 | tf_op jit(solution)/shard_map/eijc,aj->eaic/dot_general | solution.py:40
  110.8 8.3 %fusion.1 = f32[768,384]{0,1:T(8,128)S(1)} fusion(f32[3600,384]{1,0:T(8,128)S(1)} %convolution_bitcast_fusion.1, s32[3600]{0:T(1024)S(1)} %eq.35), kind=kOutput, calls=%fused_computation.10 | convolution fusion | flops 12742963200 | bytes 6723648 | tf_op jit(solution)/shard_map/dot_general | solution.py:69
  119.1 1.0 copy-done.4
  120.9 2.0 copy.55
  122.9 8.7 %collective-permute-start.1 = (f32[256,3,128]{2,1,0:T(4,128)}, f32[256,3,128]{2,1,0:T(4,128)}, u32[]{:S(2)}, u32[]{:S(2)}) collective-permute-start(f32[256,3,128]{2,1,0:T(4,128)} %copy.55), channel_id=1, source_target_pairs={{0,1},{1,2},{2,3},{3,4},{4,5},{5,6},{6,7},{7,8},{8,9},{9,10},{10,1... | collective-permute-start | bytes 1179656 | tf_op jit(solution)/shard_map/ppermute | solution.py:19
  131.6 2.1 slice.67
  133.7 2.5 copy.56
  136.1 26.5 %scatter_fusion = f32[512,3,128]{2,1,0:T(4,128)} fusion(f32[512,3,128]{2,1,0:T(4,128)} %copy.56, s32[256]{0:T(256)S(1)} %compare_select_fusion.1, f32[256,3,128]{2,1,0:T(4,128)} %collective-permute-done.1), kind=kCustom, calls=%fused_computation.4 | custom fusion | flops 98304 | bytes 1180672 | tf_op jit(solution)/shard_map/scatter-add | solution.py:76
  162.7 2.3 reshape.102
  164.9 3.2 convolution_bitcast_fusion.4
  168.2 2.0 copy.57
  170.4 40.5 %all-reduce = f32[1024]{0:T(1024)S(1)} all-reduce(f32[1024]{0:T(1024)S(1)} %dynamic-update-slice), channel_id=1, replica_groups=mesh['dom'=32] {'dom'}, use_global_device_ids=true, to_apply=%add | all-reduce | flops 1024 | bytes 8192
  210.9 71.3 %all-gather.5.cloned.1.call-done = f32[32768,128]{0,1:T(8,128)} async-done(((f32[1024,128]{0,1:T(8,128)}), f32[32768,128]{0,1:T(8,128)}) %all-gather.5.cloned.1.call-update) | async-done | bytes 16777232 | tf_op jit(solution)/shard_map/all_gather | solution.py:82
  282.2 17.7 %copy.75 = f32[16,8,32,1024]{3,2,1,0:T(8,128)} copy(f32[16,8,32,1024]{3,1,2,0:T(8,128)} %bitcast.89) | data formatting | bytes 33554432
  299.9 9.8 %bitcast_reduce_fusion.1 = f32[1024,128]{0,1:T(8,128)} fusion(f32[16,8,32,1024]{3,2,1,0:T(8,128)} %copy.75), kind=kLoop, calls=%fused_computation.7 | loop fusion | flops 4063232 | bytes 17301504 | tf_op jit(solution)/shard_map/reduce_sum | solution.py:82
  309.7 1.2 multiply_reduce_fusion.3
  310.9 1.3 divide_add_fusion
  313.0 2.1 convolution_bitcast_fusion.2
  315.1 2.3 copy.58
  317.4 2.3 reshape.103
  319.7 2.8 broadcast_multiply_fusion
  322.5 3.0 gather_fusion.2
  325.5 1.3 collective-permute-start.2
  326.8 2.7 collective-permute-done.2
  329.5 2.8 pad_maximum_fusion.1
  332.3 14.1 %gather_fusion.3 = f32[3600,3,128]{2,1,0:T(4,128)} fusion(f32[768,3,128]{2,1,0:T(4,128)} %pad_maximum_fusion.1, s32[4096]{0:T(1024)S(1)} %pad_clamp_fusion), kind=kCustom, calls=%fused_computation.3 | custom fusion | bytes 11073600 | tf_op jit(solution)/shard_map/gather | solution.py:68
  346.4 8.2 %fusion.4 = f32[3,450,3,128]{3,0,2,1:T(4,128)S(1)} fusion(f32[450,8,3,128]{3,2,1,0:T(4,128)} %bitcast.87), kind=kOutput, calls=%fused_computation.15 | convolution fusion | flops 49766544 | bytes 7603200 | tf_op jit(solution)/shard_map/eaic,aj->eijc/dot_general | solution.py:28
  354.6 1.1 fusion.8
  356.6 2.2 multiply_reduce_fusion
  359.0 4.6 multiply_add_fusion
  363.5 6.6 %convolution_bitcast_fusion = f32[3600,384]{1,0:T(8,128)S(1)} fusion(f32[450,3,3,128]{3,1,2,0:T(4,128)S(1)} %multiply_add_fusion), kind=kOutput, calls=%fused_computation.11 | convolution fusion | flops 49766544 | bytes 7603200 | tf_op jit(solution)/shard_map/eijc,aj->eaic/dot_general | solution.py:40
  370.1 8.3 %fusion = f32[768,384]{0,1:T(8,128)S(1)} fusion(f32[3600,384]{1,0:T(8,128)S(1)} %convolution_bitcast_fusion, s32[3600]{0:T(1024)S(1)} %eq.35), kind=kOutput, calls=%fused_computation.9 | convolution fusion | flops 12742963200 | bytes 6723648 | tf_op jit(solution)/shard_map/dot_general | solution.py:69
  378.5 1.0 copy-done.5
  379.5 1.0 copy.63
  380.5 9.7 %collective-permute-start.3 = (f32[256,3,128]{2,1,0:T(4,128)}, f32[256,3,128]{2,1,0:T(4,128)}, u32[]{:S(2)}, u32[]{:S(2)}) collective-permute-start(f32[256,3,128]{2,1,0:T(4,128)} %copy.63), channel_id=1, source_target_pairs={{0,1},{1,2},{2,3},{3,4},{4,5},{5,6},{6,7},{7,8},{8,9},{9,10},{10,1... | collective-permute-start | bytes 1179656 | tf_op jit(solution)/shard_map/ppermute | solution.py:19
  390.1 2.1 slice.72
  392.2 2.5 copy.64
  394.7 26.6 %scatter_fusion.1 = f32[512,3,128]{2,1,0:T(4,128)} fusion(f32[512,3,128]{2,1,0:T(4,128)} %copy.64, s32[256]{0:T(256)S(1)} %compare_select_fusion.1, f32[256,3,128]{2,1,0:T(4,128)} %collective-permute-done.3), kind=kCustom, calls=%fused_computation.5 | custom fusion | flops 98304 | bytes 1180672 | tf_op jit(solution)/shard_map/scatter-add | solution.py:76
  421.2 2.3 reshape.105
  423.5 1.5 sub.25
  425.0 0.9 copy-done.2
  425.8 1.8 convolution_bitcast_fusion.3
  427.7 117.4 %all-gather.7.cloned.1.call-done = f32[32768,128]{0,1:T(8,128)} async-done(((f32[1024,128]{0,1:T(8,128)}), f32[32768,128]{0,1:T(8,128)}) %all-gather.7.cloned.1.call-update) | async-done | bytes 16777232 | tf_op jit(solution)/shard_map/all_gather | solution.py:82
  545.1 17.7 %copy.76 = f32[16,8,32,1024]{3,2,1,0:T(8,128)} copy(f32[16,8,32,1024]{3,1,2,0:T(8,128)} %bitcast.90) | data formatting | bytes 33554432
  562.8 9.8 %bitcast_reduce_fusion = f32[1024,128]{0,1:T(8,128)} fusion(f32[16,8,32,1024]{3,2,1,0:T(8,128)} %copy.76), kind=kLoop, calls=%fused_computation.6 | loop fusion | flops 4063232 | bytes 17301504 | tf_op jit(solution)/shard_map/reduce_sum | solution.py:82
  572.6 1.2 multiply_reduce_fusion.2
  573.8 1.0 dynamic-slice_add_fusion
  (48 shorter events, 6.5 us)
Async XLA Ops:
  7.2 47.6 %copy-start = (bf16[1536,1024]{1,0:T(8,128)(2,1)S(1)}, bf16[1536,1024]{1,0:T(8,128)(2,1)}, u32[]{:S(2)}) copy-start(bf16[1536,1024]{1,0:T(8,128)(2,1)} %param.9) | copy-start | bytes 9437188
  7.2 275.0 %all-gather.5.cloned.1.call-start = ((), (), s32[]{:S(2)}) async-start(), calls=%async_computation | async-start | bytes 17301504 | tf_op jit(solution)/shard_map/all_gather | solution.py:82
  54.0 0.8 copy-start.1
  56.7 9.4 %copy-start.6 = (s32[450,8]{0,1:T(8,128)S(1)}, s32[450,8]{0,1:T(8,128)}, u32[]{:S(2)}) copy-start(s32[450,8]{0,1:T(8,128)} %param.13) | copy-start | bytes 43204
  56.7 13.3 %copy-start.8 = (s32[450]{0:T(512)S(1)}, s32[450]{0:T(512)}, u32[]{:S(2)}) copy-start(s32[450]{0:T(512)} %param.15) | copy-start | bytes 5404
  64.8 5.2 collective-permute-start
  110.7 20.8 %copy-start.7 = (f32[12]{0:T(128)S(1)}, f32[12]{0:T(128)}, u32[]{:S(2)}) copy-start(f32[12]{0:T(128)} %param.10) | copy-start | bytes 148
  119.1 1.0 copy-start.4
  122.9 13.3 %collective-permute-start.1 = (f32[256,3,128]{2,1,0:T(4,128)}, f32[256,3,128]{2,1,0:T(4,128)}, u32[]{:S(2)}, u32[]{:S(2)}) collective-permute-start(f32[256,3,128]{2,1,0:T(4,128)} %copy.55), channel_id=1, source_target_pairs={{0,1},{1,2},{2,3},{3,4},{4,5},{5,6},{6,7},{7,8},{8,9},{9,10},{10,1... | collective-permute-start | bytes 1179656 | tf_op jit(solution)/shard_map/ppermute | solution.py:19
  164.9 5.3 copy-start.9
  168.2 377.0 %all-gather.7.cloned.1.call-start = ((), (), s32[]{:S(2)}) async-start(), calls=%async_computation.1 | async-start | bytes 17301504 | tf_op jit(solution)/shard_map/all_gather | solution.py:82
  312.2 0.8 copy-start.3
  325.5 4.0 collective-permute-start.2
  378.5 1.0 copy-start.5
  380.5 14.2 %collective-permute-start.3 = (f32[256,3,128]{2,1,0:T(4,128)}, f32[256,3,128]{2,1,0:T(4,128)}, u32[]{:S(2)}, u32[]{:S(2)}) collective-permute-start(f32[256,3,128]{2,1,0:T(4,128)} %copy.63), channel_id=1, source_target_pairs={{0,1},{1,2},{2,3},{3,4},{4,5},{5,6},{6,7},{7,8},{8,9},{9,10},{10,1... | collective-permute-start | bytes 1179656 | tf_op jit(solution)/shard_map/ppermute | solution.py:19
  425.0 0.9 copy-start.2
Sparse Core Ops, SparseCore 0:
  168.3 113.8 all-gather.4
  427.8 117.2 all-gather.6
